TPU v7x, 32 devices: a whole 2x2x4 slice. The times are simulated.
32 devices in a mesh: loan: 8 (over y, x, core), path: 4 (over z).
Axes of the slice: x: 2, y: 2, z: 4, core: 2. Of those that a mesh axis runs over, the one named last changes fastest.
Arguments:
- price_moves: bfloat16 [12, 416, 512], P(None, 'loan', 'path'), may hold values from -0.1796875 to 0.1796875
- block_regions: int32 [16, 32], P('loan'), may hold values from 0 to 415
- region_slot: int32 [4096], P('loan'), may hold values from 0 to 31
- block_pools: int32 [16, 32], P('loan'), may hold values from 0 to 511, as said below
- pool_slot: int32 [4096], P('loan'), may hold values from 0 to 31, as said below
- init_state: int32 [4096], P('loan'), may hold values from 0 to 5
- balance: float32 [4096], P('loan'), may hold values from 0.5 to 2
- loan_to_value: float32 [4096], P('loan'), may hold values from 0.5 to 1.3
- hazard_base: float32 [2, 6], replicated, may hold values from -4 to -1
- hazard_slope: float32 [2, 6], replicated, may hold values from 1 to 4
- attach_bps: int32 [512, 6], P('loan'), may hold values from 0 to 2995, as said below
Outputs:
- expected_loss: float32 [6, 3, 512], P(None, None, 'loan')
- path_loss: float32 [6, 512, 512], P(None, 'loan', 'path')
Inputs may be any that keep to these rules, and one draw needn't show every extreme that they name: `block_pools`: over all blocks' lists every pool appears exactly once. The lists of the blocks held by one index of loan name exactly 64 // 8 pools of every owner, owner k being the index of loan that holds pools k * 64 to (k + 1) * 64 - 1. `pool_slot`: every aligned block of 256 loans uses each position of its pool list at least once. `attach_bps`: each row starts at 0 and rises by 100 to 599 from one tranche to the next.
All inputs are finite; a program needn't handle non-finite values.
Results may differ from a plain program's by a relative error of at most 0.0003.
Values may be sent and summed in bfloat16 or wider, within the bound.
No kernel may reach another device: no remote copies, remote signals or barrier semaphores. Data moves between devices by JAX's collectives and lax.ppermute only.
A program may use at most 64 MiB of HBM per device.

v0:
```python
import jax
import jax.numpy as jnp
from jax import lax
from jax.sharding import PartitionSpec as P

BLOCK = 256
stress_scale = 0.3


def roll_months(
    routed, path_place, path_count, log_value, initial, balance, hazard_base, hazard_slope
):
    months = routed.shape[0]
    month_place = (jnp.arange(months, dtype=jnp.float32) + 1.0) / months
    stress_path = (
        stress_scale * ((path_place + 0.5) / path_count)[None, :, None] * month_place[:, None, None]
    )
    cumulated = jnp.cumsum(routed, axis=0) - stress_path
    level = log_value[None, None, :] - cumulated
    start_state = jnp.broadcast_to(
        initial[:, None, :], (initial.shape[0], routed.shape[1], routed.shape[2])
    )
    loss_start = jnp.zeros(routed.shape[1:], jnp.float32)

    def month_step(state_pair, ltv_now):
        state, loss_sum = state_pair
        roll_rate = jax.nn.sigmoid(
            hazard_base[0][:, None, None] + hazard_slope[0][:, None, None] * ltv_now[None]
        )
        cure_rate = jax.nn.sigmoid(
            hazard_base[1][:, None, None] - hazard_slope[1][:, None, None] * ltv_now[None]
        )
        stay_rate = (1.0 - roll_rate) * (1.0 - cure_rate)
        forward = state * roll_rate
        backward = state * (1.0 - roll_rate) * cure_rate
        first_state = state[0] * stay_rate[0] + jnp.sum(backward[1:], axis=0)
        rest_state = forward[:-1] + state[1:] * stay_rate[1:]
        updated = jnp.concatenate([first_state[None], rest_state], axis=0)
        severity = 0.1 + 0.5 * jax.nn.sigmoid(3.0 * ltv_now)
        loss_next = loss_sum + balance[None, :] * severity * forward[-1]
        return ((updated, loss_next), loss_next)

    state_pair, history = lax.scan(month_step, (start_state, loss_start), level)
    return history[3::4]


def lookup(lookup_table, positions):
    matches = positions[:, None] == jnp.arange(lookup_table.shape[0], dtype=jnp.int32)[None, :]
    return jnp.sum(jnp.where(matches, lookup_table[None, :], 0), axis=1)


def shards(
    price_moves,
    block_regions,
    region_slot,
    block_pools,
    pool_slot,
    init_state,
    balance,
    loan_to_value,
    hazard_base,
    hazard_slope,
    attach_bps,
):
    loan_dev = region_slot.shape[0]
    months, metro_dev, path_dev = price_moves.shape
    pool_dev = attach_bps.shape[0]
    dates = months // 4
    block_index = jnp.arange(loan_dev, dtype=jnp.int32) // BLOCK
    metro_id = lookup(block_regions.reshape(-1), block_index * block_regions.shape[1] + region_slot)
    slot_id = block_index * block_pools.shape[1] + pool_slot
    listed_pools = block_pools.reshape(-1)
    shard = lax.all_gather(price_moves, "loan", axis=1, tiled=True)
    chooser = (metro_id[None, :] == jnp.arange(shard.shape[1], dtype=jnp.int32)[:, None]).astype(
        jnp.bfloat16
    )
    routed = jnp.einsum("mrp,rl->mpl", shard, chooser, preferred_element_type=jnp.float32)
    path_count = path_dev * lax.axis_size("path")
    path_place = (lax.axis_index("path") * path_dev + jnp.arange(path_dev, dtype=jnp.int32)).astype(
        jnp.float32
    )
    initial = (
        init_state[None, :] == jnp.arange(hazard_base.shape[1], dtype=jnp.int32)[:, None]
    ).astype(jnp.float32)
    losses = roll_months(
        routed,
        path_place,
        float(path_count),
        jnp.log(loan_to_value),
        initial,
        balance,
        hazard_base,
        hazard_slope,
    )
    loss_rows = losses.reshape(dates * path_dev, loan_dev)
    contract = (((1,), (1,)), ((), ()))
    slot_count = listed_pools.shape[0]
    members = (slot_id[None, :] == jnp.arange(slot_count, dtype=jnp.int32)[:, None]).astype(
        jnp.float32
    )
    slot_loss = lax.dot_general(
        members,
        loss_rows,
        contract,
        precision=lax.Precision.HIGHEST,
        preferred_element_type=jnp.float32,
    )
    slot_balance = jnp.dot(
        members, balance, precision=lax.Precision.HIGHEST, preferred_element_type=jnp.float32
    )
    ranking = jnp.argsort(listed_pools // pool_dev, stable=True)
    outgoing = (
        slot_loss[ranking],
        slot_balance[ranking],
        listed_pools[ranking].astype(jnp.float32),
    )
    got_loss, got_balance, got_pool = (
        lax.all_to_all(outgoing[0], "loan", split_axis=0, concat_axis=0, tiled=True),
        lax.all_to_all(outgoing[1], "loan", split_axis=0, concat_axis=0, tiled=True),
        lax.all_to_all(outgoing[2], "loan", split_axis=0, concat_axis=0, tiled=True),
    )
    local_pool = got_pool - (lax.axis_index("loan") * pool_dev).astype(jnp.float32)
    placing = (
        local_pool[None, :] == jnp.arange(pool_dev, dtype=jnp.int32)[:, None].astype(jnp.float32)
    ).astype(jnp.float32)
    pool_loss = jnp.dot(
        placing, got_loss, precision=lax.Precision.HIGHEST, preferred_element_type=jnp.float32
    )
    notional = jnp.dot(
        placing, got_balance, precision=lax.Precision.HIGHEST, preferred_element_type=jnp.float32
    )
    attach = attach_bps.astype(jnp.float32) / 10000.0
    detach = jnp.concatenate([attach[:, 1:], jnp.ones((pool_dev, 1), jnp.float32)], axis=1)
    ratio = pool_loss.reshape(pool_dev, dates, path_dev) / notional[:, None, None]
    lower = attach.T[:, :, None, None]
    height = (detach - attach).T[:, :, None, None]
    shares = jnp.clip((ratio[None] - lower) / height, 0.0, 1.0)
    partial_value = jnp.sum(shares, axis=3).transpose(0, 2, 1)
    expected_loss = lax.psum(partial_value, "path") / path_count
    return (expected_loss, shares[:, :, -1, :])


def solution(mesh):
    in_specs = (
        P(None, "loan", "path"),
        P("loan", None),
        P("loan"),
        P("loan", None),
        P("loan"),
        P("loan"),
        P("loan"),
        P("loan"),
        P(),
        P(),
        P("loan", None),
    )
    out_specs = (P(None, None, "loan"), P(None, "loan", "path"))
    return jax.shard_map(shards, mesh=mesh, in_specs=in_specs, out_specs=out_specs, check_vma=False)
```

profile of v0, /device:TPU:0, one launch (start us, length us, event | category | flops | bytes accessed | tf_op | source)
XLA Modules:
  0.0 173.0 jit_solution(12231268295599842908)
XLA Ops:
  13.2 5.2 %all-to-all-start = ((f32[8,8,1]{1,2,0:T(1,128)}), f32[8,8,1]{1,2,0:T(1,128)S(1)}, u32[]{:S(2)}, u32[]{:S(2)}) async-start(f32[8,8,1]{1,2,0:T(1,128)} %bitcast), calls=%async_computation | async-start | bytes 8192 | tf_op jit(solution)/shard_map/all_to_all | solution.py:120
  23.0 3.3 %all-to-all-start.2 = ((f32[8,8,1]{1,2,0:T(1,128)}), f32[8,8,1]{1,2,0:T(1,128)S(1)}, u32[]{:S(2)}, u32[]{:S(2)}) async-start(f32[8,8,1]{1,2,0:T(1,128)} %bitcast.10), calls=%async_computation.2 | async-start | bytes 8192 | tf_op jit(solution)/shard_map/all_to_all | solution.py:119
  26.5 4.4 %all-to-all-done.2 = f32[8,8,1]{1,2,0:T(1,128)S(1)} async-done(((f32[8,8,1]{1,2,0:T(1,128)}), f32[8,8,1]{1,2,0:T(1,128)S(1)}, u32[]{:S(2)}, u32[]{:S(2)}) %all-to-all-start.2) | async-done | bytes 288 | tf_op jit(solution)/shard_map/all_to_all | solution.py:119
  32.2 6.6 %all-gather.2.cloned.1.call-done = bf16[12,416,128]{2,0,1:T(8,128)(2,1)} async-done(((bf16[12,52,128]{2,0,1:T(8,128)(2,1)}), bf16[12,416,128]{2,0,1:T(8,128)(2,1)}) %all-gather.2.cloned.1.call-update) | async-done | bytes 1277968 | tf_op jit(solution)/shard_map/all_gather | solution.py:73
  38.8 2.5 %fusion.9 = f32[512,12,128]{2,0,1:T(8,128)S(1)} fusion(bf16[12,416,128]{2,0,1:T(8,128)(2,1)} %all-gather.2.cloned.1.call-done, s32[512]{0:T(512)S(1)} %select_reduce_fusion), kind=kOutput, calls=%fused_computation.28 | convolution fusion | flops 654524416 | bytes 4425728 | tf_op jit(solution)/shard_map/mrp,rl->mpl/dot_general | solution.py:77
  44.1 89.9 %while.15 = (s32[]{:T(128)}, f32[6,128,512]{2,1,0:T(8,128)S(1)}, f32[128,512]{1,0:T(8,128)}, f32[12,128,512]{2,1,0:T(8,128)}, f32[2,6]{1,0:T(2,128)S(1)}, /*inde...) while((s32[]{:T(128)}, f32[6,128,512]{2,1,0:T(8,128)S(1)}, ...), condition=%wide.region_5.6_spmd.clone, body=%wide.region_3.5_spmd.clone.sunk | while | flops 8257539 | bytes 34343880 | solution.py:43
  46.4 2.7 %fusion.43 = (f32[128,512]{1,0:T(8,128)}, f32[5,128,512]{2,1,0:T(8,128)}) fusion(f32[6,128,512]{2,1,0:T(8,128)S(1)} %get-tuple-element.209, f32[6,128,512]{2,1,0:T(8,128)S(1)} %get-tuple-element.210, f32[6,128,512]{2,1,0:T(8,128)S(1)} %get-tuple-element.229, f32[6,128,512]{2,1,0:T(8,128)S(1)} %get-tuple-element.211, ...), kind=kLoop, calls=%fused_computation.10.clone.1 | loop fusion | flops 1572864 | bytes 8126464 | tf_op jit(solution)/shard_map/while/body/eval_jaxpr/reduce_sum | solution.py:36
  53.9 2.7 %fusion.43 = (f32[128,512]{1,0:T(8,128)}, f32[5,128,512]{2,1,0:T(8,128)}) fusion(f32[6,128,512]{2,1,0:T(8,128)S(1)} %get-tuple-element.209, f32[6,128,512]{2,1,0:T(8,128)S(1)} %get-tuple-element.210, f32[6,128,512]{2,1,0:T(8,128)S(1)} %get-tuple-element.229, f32[6,128,512]{2,1,0:T(8,128)S(1)} %get-tuple-element.211, ...), kind=kLoop, calls=%fused_computation.10.clone.1 | loop fusion | flops 1572864 | bytes 8126464 | tf_op jit(solution)/shard_map/while/body/eval_jaxpr/reduce_sum | solution.py:36
  56.6 2.2 %bitcast_dynamic-update-slice_fusion.2 = (f32[12,128,512]{2,1,0:T(8,128)}, f32[128,512]{1,0:T(8,128)}, f32[1,128,512]{2,1,0:T(8,128)S(1)}) fusion(f32[12,128,512]{2,1,0:T(8,128)} %get-tuple-element.231, s32[]{:T(128)} %get-tuple-element.228, f32[6,128,512]{2,1,0:T(8,128)S(1)} %get-tuple-element.212, f32[1,128,512]{2,1,0:T(8,128)S(1)} %copy.39, ...), kind=kLoop, calls=%fused_computation.19.clone.1 | loop fusion | flops 786432 | bytes 2361857 | tf_op jit(solution)/shard_map/while/body/jit(dynamic_update_index_in_dim)/dynamic_update_slice | solution.py:43
  61.4 2.7 %fusion.43 = (f32[128,512]{1,0:T(8,128)}, f32[5,128,512]{2,1,0:T(8,128)}) fusion(f32[6,128,512]{2,1,0:T(8,128)S(1)} %get-tuple-element.209, f32[6,128,512]{2,1,0:T(8,128)S(1)} %get-tuple-element.210, f32[6,128,512]{2,1,0:T(8,128)S(1)} %get-tuple-element.229, f32[6,128,512]{2,1,0:T(8,128)S(1)} %get-tuple-element.211, ...), kind=kLoop, calls=%fused_computation.10.clone.1 | loop fusion | flops 1572864 | bytes 8126464 | tf_op jit(solution)/shard_map/while/body/eval_jaxpr/reduce_sum | solution.py:36
  68.9 2.7 %fusion.43 = (f32[128,512]{1,0:T(8,128)}, f32[5,128,512]{2,1,0:T(8,128)}) fusion(f32[6,128,512]{2,1,0:T(8,128)S(1)} %get-tuple-element.209, f32[6,128,512]{2,1,0:T(8,128)S(1)} %get-tuple-element.210, f32[6,128,512]{2,1,0:T(8,128)S(1)} %get-tuple-element.229, f32[6,128,512]{2,1,0:T(8,128)S(1)} %get-tuple-element.211, ...), kind=kLoop, calls=%fused_computation.10.clone.1 | loop fusion | flops 1572864 | bytes 8126464 | tf_op jit(solution)/shard_map/while/body/eval_jaxpr/reduce_sum | solution.py:36
  76.4 2.7 %fusion.43 = (f32[128,512]{1,0:T(8,128)}, f32[5,128,512]{2,1,0:T(8,128)}) fusion(f32[6,128,512]{2,1,0:T(8,128)S(1)} %get-tuple-element.209, f32[6,128,512]{2,1,0:T(8,128)S(1)} %get-tuple-element.210, f32[6,128,512]{2,1,0:T(8,128)S(1)} %get-tuple-element.229, f32[6,128,512]{2,1,0:T(8,128)S(1)} %get-tuple-element.211, ...), kind=kLoop, calls=%fused_computation.10.clone.1 | loop fusion | flops 1572864 | bytes 8126464 | tf_op jit(solution)/shard_map/while/body/eval_jaxpr/reduce_sum | solution.py:36
  79.1 2.2 %bitcast_dynamic-update-slice_fusion.2 = (f32[12,128,512]{2,1,0:T(8,128)}, f32[128,512]{1,0:T(8,128)}, f32[1,128,512]{2,1,0:T(8,128)S(1)}) fusion(f32[12,128,512]{2,1,0:T(8,128)} %get-tuple-element.231, s32[]{:T(128)} %get-tuple-element.228, f32[6,128,512]{2,1,0:T(8,128)S(1)} %get-tuple-element.212, f32[1,128,512]{2,1,0:T(8,128)S(1)} %copy.39, ...), kind=kLoop, calls=%fused_computation.19.clone.1 | loop fusion | flops 786432 | bytes 2361857 | tf_op jit(solution)/shard_map/while/body/jit(dynamic_update_index_in_dim)/dynamic_update_slice | solution.py:43
  83.9 2.7 %fusion.43 = (f32[128,512]{1,0:T(8,128)}, f32[5,128,512]{2,1,0:T(8,128)}) fusion(f32[6,128,512]{2,1,0:T(8,128)S(1)} %get-tuple-element.209, f32[6,128,512]{2,1,0:T(8,128)S(1)} %get-tuple-element.210, f32[6,128,512]{2,1,0:T(8,128)S(1)} %get-tuple-element.229, f32[6,128,512]{2,1,0:T(8,128)S(1)} %get-tuple-element.211, ...), kind=kLoop, calls=%fused_computation.10.clone.1 | loop fusion | flops 1572864 | bytes 8126464 | tf_op jit(solution)/shard_map/while/body/eval_jaxpr/reduce_sum | solution.py:36
  91.4 2.7 %fusion.43 = (f32[128,512]{1,0:T(8,128)}, f32[5,128,512]{2,1,0:T(8,128)}) fusion(f32[6,128,512]{2,1,0:T(8,128)S(1)} %get-tuple-element.209, f32[6,128,512]{2,1,0:T(8,128)S(1)} %get-tuple-element.210, f32[6,128,512]{2,1,0:T(8,128)S(1)} %get-tuple-element.229, f32[6,128,512]{2,1,0:T(8,128)S(1)} %get-tuple-element.211, ...), kind=kLoop, calls=%fused_computation.10.clone.1 | loop fusion | flops 1572864 | bytes 8126464 | tf_op jit(solution)/shard_map/while/body/eval_jaxpr/reduce_sum | solution.py:36
  98.9 2.7 %fusion.43 = (f32[128,512]{1,0:T(8,128)}, f32[5,128,512]{2,1,0:T(8,128)}) fusion(f32[6,128,512]{2,1,0:T(8,128)S(1)} %get-tuple-element.209, f32[6,128,512]{2,1,0:T(8,128)S(1)} %get-tuple-element.210, f32[6,128,512]{2,1,0:T(8,128)S(1)} %get-tuple-element.229, f32[6,128,512]{2,1,0:T(8,128)S(1)} %get-tuple-element.211, ...), kind=kLoop, calls=%fused_computation.10.clone.1 | loop fusion | flops 1572864 | bytes 8126464 | tf_op jit(solution)/shard_map/while/body/eval_jaxpr/reduce_sum | solution.py:36
  101.6 2.3 %bitcast_dynamic-update-slice_fusion.2 = (f32[12,128,512]{2,1,0:T(8,128)}, f32[128,512]{1,0:T(8,128)}, f32[1,128,512]{2,1,0:T(8,128)S(1)}) fusion(f32[12,128,512]{2,1,0:T(8,128)} %get-tuple-element.231, s32[]{:T(128)} %get-tuple-element.228, f32[6,128,512]{2,1,0:T(8,128)S(1)} %get-tuple-element.212, f32[1,128,512]{2,1,0:T(8,128)S(1)} %copy.39, ...), kind=kLoop, calls=%fused_computation.19.clone.1 | loop fusion | flops 786432 | bytes 2361857 | tf_op jit(solution)/shard_map/while/body/jit(dynamic_update_index_in_dim)/dynamic_update_slice | solution.py:43
  106.4 2.7 %fusion.43 = (f32[128,512]{1,0:T(8,128)}, f32[5,128,512]{2,1,0:T(8,128)}) fusion(f32[6,128,512]{2,1,0:T(8,128)S(1)} %get-tuple-element.209, f32[6,128,512]{2,1,0:T(8,128)S(1)} %get-tuple-element.210, f32[6,128,512]{2,1,0:T(8,128)S(1)} %get-tuple-element.229, f32[6,128,512]{2,1,0:T(8,128)S(1)} %get-tuple-element.211, ...), kind=kLoop, calls=%fused_computation.10.clone.1 | loop fusion | flops 1572864 | bytes 8126464 | tf_op jit(solution)/shard_map/while/body/eval_jaxpr/reduce_sum | solution.py:36
  113.9 2.7 %fusion.43 = (f32[128,512]{1,0:T(8,128)}, f32[5,128,512]{2,1,0:T(8,128)}) fusion(f32[6,128,512]{2,1,0:T(8,128)S(1)} %get-tuple-element.209, f32[6,128,512]{2,1,0:T(8,128)S(1)} %get-tuple-element.210, f32[6,128,512]{2,1,0:T(8,128)S(1)} %get-tuple-element.229, f32[6,128,512]{2,1,0:T(8,128)S(1)} %get-tuple-element.211, ...), kind=kLoop, calls=%fused_computation.10.clone.1 | loop fusion | flops 1572864 | bytes 8126464 | tf_op jit(solution)/shard_map/while/body/eval_jaxpr/reduce_sum | solution.py:36
  121.4 2.7 %fusion.43 = (f32[128,512]{1,0:T(8,128)}, f32[5,128,512]{2,1,0:T(8,128)}) fusion(f32[6,128,512]{2,1,0:T(8,128)S(1)} %get-tuple-element.209, f32[6,128,512]{2,1,0:T(8,128)S(1)} %get-tuple-element.210, f32[6,128,512]{2,1,0:T(8,128)S(1)} %get-tuple-element.229, f32[6,128,512]{2,1,0:T(8,128)S(1)} %get-tuple-element.211, ...), kind=kLoop, calls=%fused_computation.10.clone.1 | loop fusion | flops 1572864 | bytes 8126464 | tf_op jit(solution)/shard_map/while/body/eval_jaxpr/reduce_sum | solution.py:36
  128.9 2.7 %fusion.43 = (f32[128,512]{1,0:T(8,128)}, f32[5,128,512]{2,1,0:T(8,128)}) fusion(f32[6,128,512]{2,1,0:T(8,128)S(1)} %get-tuple-element.209, f32[6,128,512]{2,1,0:T(8,128)S(1)} %get-tuple-element.210, f32[6,128,512]{2,1,0:T(8,128)S(1)} %get-tuple-element.229, f32[6,128,512]{2,1,0:T(8,128)S(1)} %get-tuple-element.211, ...), kind=kLoop, calls=%fused_computation.10.clone.1 | loop fusion | flops 1572864 | bytes 8126464 | tf_op jit(solution)/shard_map/while/body/eval_jaxpr/reduce_sum | solution.py:36
  137.0 3.4 %all-to-all-start.1 = ((f32[8,8,384]{2,1,0:T(8,128)}), f32[8,8,384]{2,1,0:T(8,128)S(1)}, u32[]{:S(2)}, u32[]{:S(2)}) async-start(f32[8,8,384]{2,1,0:T(8,128)} %bitcast.5), calls=%async_computation.1 | async-start | bytes 196608 | tf_op jit(solution)/shard_map/all_to_all | solution.py:118
  140.6 4.9 %all-to-all-done.1 = f32[8,8,384]{2,1,0:T(8,128)S(1)} async-done(((f32[8,8,384]{2,1,0:T(8,128)}), f32[8,8,384]{2,1,0:T(8,128)S(1)}, u32[]{:S(2)}, u32[]{:S(2)}) %all-to-all-start.1) | async-done | bytes 98336 | tf_op jit(solution)/shard_map/all_to_all | solution.py:118
  146.8 18.7 %psum.7 = f32[6,3,64]{2,0,1:T(8,128)S(1)} all-reduce(f32[6,3,64]{2,0,1:T(8,128)S(1)} %bitcast.74), channel_id=1, replica_groups=mesh['loan'=8,'path'=4] {'path'}, use_global_device_ids=true, to_apply=%region_7.8 | all-reduce | flops 1152 | bytes 9216 | tf_op jit(solution)/shard_map/psum | solution.py:139
  (192 shorter events, 69.3 us)
Async XLA Ops:
  7.2 14.3 %copy-start.9 = (s32[2,32]{1,0:T(2,128)S(1)}, s32[2,32]{1,0:T(2,128)}, u32[]{:S(2)}) copy-start(s32[2,32]{1,0:T(2,128)} %param.14) | copy-start | bytes 772
  7.2 14.3 %copy-start.5 = (s32[64,6]{0,1:T(8,128)S(1)}, s32[64,6]{0,1:T(8,128)}, u32[]{:S(2)}) copy-start(s32[64,6]{0,1:T(8,128)} %param.23) | copy-start | bytes 4612
  7.2 14.4 %copy-start.7 = (s32[512]{0:T(512)S(1)}, s32[512]{0:T(512)}, u32[]{:S(2)}) copy-start(s32[512]{0:T(512)} %param.15) | copy-start | bytes 6148
  7.2 14.6 %copy-start.6 = (s32[512]{0:T(512)S(1)}, s32[512]{0:T(512)}, u32[]{:S(2)}) copy-start(s32[512]{0:T(512)} %param.18) | copy-start | bytes 6148
  7.2 14.6 %copy-start.8 = (f32[512]{0:T(512)S(1)}, f32[512]{0:T(512)}, u32[]{:S(2)}) copy-start(f32[512]{0:T(512)} %param.20) | copy-start | bytes 6148
  7.2 31.6 %all-gather.2.cloned.1.call-start = ((), (), s32[]{:S(2)}) async-start(), calls=%async_computation.3 | async-start | bytes 1916928 | tf_op jit(solution)/shard_map/all_gather | solution.py:73
  13.2 9.8 %all-to-all-start = ((f32[8,8,1]{1,2,0:T(1,128)}), f32[8,8,1]{1,2,0:T(1,128)S(1)}, u32[]{:S(2)}, u32[]{:S(2)}) async-start(f32[8,8,1]{1,2,0:T(1,128)} %bitcast), calls=%async_computation | async-start | bytes 8192 | tf_op jit(solution)/shard_map/all_to_all | solution.py:120
  23.0 7.9 %all-to-all-start.2 = ((f32[8,8,1]{1,2,0:T(1,128)}), f32[8,8,1]{1,2,0:T(1,128)S(1)}, u32[]{:S(2)}, u32[]{:S(2)}) async-start(f32[8,8,1]{1,2,0:T(1,128)} %bitcast.10), calls=%async_computation.2 | async-start | bytes 8192 | tf_op jit(solution)/shard_map/all_to_all | solution.py:119
  46.4 2.8 %copy-start = (f32[6,128,512]{2,1,0:T(8,128)}, f32[6,128,512]{2,1,0:T(8,128)S(1)}, u32[]{:S(2)}) copy-start(f32[6,128,512]{2,1,0:T(8,128)S(1)} %get-tuple-element.211) | copy-start | bytes 4718596 | tf_op jit(solution)/shard_map/while
  53.9 2.8 %copy-start = (f32[6,128,512]{2,1,0:T(8,128)}, f32[6,128,512]{2,1,0:T(8,128)S(1)}, u32[]{:S(2)}) copy-start(f32[6,128,512]{2,1,0:T(8,128)S(1)} %get-tuple-element.211) | copy-start | bytes 4718596 | tf_op jit(solution)/shard_map/while
  56.6 2.2 %copy-start.1 = (f32[5,128,512]{2,1,0:T(8,128)S(1)}, f32[5,128,512]{2,1,0:T(8,128)}, u32[]{:S(2)}) copy-start(f32[5,128,512]{2,1,0:T(8,128)} %get-tuple-element.213) | copy-start | bytes 3932164 | tf_op jit(solution)/shard_map/while
  61.4 2.8 %copy-start = (f32[6,128,512]{2,1,0:T(8,128)}, f32[6,128,512]{2,1,0:T(8,128)S(1)}, u32[]{:S(2)}) copy-start(f32[6,128,512]{2,1,0:T(8,128)S(1)} %get-tuple-element.211) | copy-start | bytes 4718596 | tf_op jit(solution)/shard_map/while
  64.1 2.2 %copy-start.1 = (f32[5,128,512]{2,1,0:T(8,128)S(1)}, f32[5,128,512]{2,1,0:T(8,128)}, u32[]{:S(2)}) copy-start(f32[5,128,512]{2,1,0:T(8,128)} %get-tuple-element.213) | copy-start | bytes 3932164 | tf_op jit(solution)/shard_map/while
  68.9 2.8 %copy-start = (f32[6,128,512]{2,1,0:T(8,128)}, f32[6,128,512]{2,1,0:T(8,128)S(1)}, u32[]{:S(2)}) copy-start(f32[6,128,512]{2,1,0:T(8,128)S(1)} %get-tuple-element.211) | copy-start | bytes 4718596 | tf_op jit(solution)/shard_map/while
  76.4 2.8 %copy-start = (f32[6,128,512]{2,1,0:T(8,128)}, f32[6,128,512]{2,1,0:T(8,128)S(1)}, u32[]{:S(2)}) copy-start(f32[6,128,512]{2,1,0:T(8,128)S(1)} %get-tuple-element.211) | copy-start | bytes 4718596 | tf_op jit(solution)/shard_map/while
  83.9 2.8 %copy-start = (f32[6,128,512]{2,1,0:T(8,128)}, f32[6,128,512]{2,1,0:T(8,128)S(1)}, u32[]{:S(2)}) copy-start(f32[6,128,512]{2,1,0:T(8,128)S(1)} %get-tuple-element.211) | copy-start | bytes 4718596 | tf_op jit(solution)/shard_map/while
  91.4 2.8 %copy-start = (f32[6,128,512]{2,1,0:T(8,128)}, f32[6,128,512]{2,1,0:T(8,128)S(1)}, u32[]{:S(2)}) copy-start(f32[6,128,512]{2,1,0:T(8,128)S(1)} %get-tuple-element.211) | copy-start | bytes 4718596 | tf_op jit(solution)/shard_map/while
  98.9 2.8 %copy-start = (f32[6,128,512]{2,1,0:T(8,128)}, f32[6,128,512]{2,1,0:T(8,128)S(1)}, u32[]{:S(2)}) copy-start(f32[6,128,512]{2,1,0:T(8,128)S(1)} %get-tuple-element.211) | copy-start | bytes 4718596 | tf_op jit(solution)/shard_map/while
  101.6 2.3 %copy-start.1 = (f32[5,128,512]{2,1,0:T(8,128)S(1)}, f32[5,128,512]{2,1,0:T(8,128)}, u32[]{:S(2)}) copy-start(f32[5,128,512]{2,1,0:T(8,128)} %get-tuple-element.213) | copy-start | bytes 3932164 | tf_op jit(solution)/shard_map/while
  106.4 2.8 %copy-start = (f32[6,128,512]{2,1,0:T(8,128)}, f32[6,128,512]{2,1,0:T(8,128)S(1)}, u32[]{:S(2)}) copy-start(f32[6,128,512]{2,1,0:T(8,128)S(1)} %get-tuple-element.211) | copy-start | bytes 4718596 | tf_op jit(solution)/shard_map/while
  113.9 2.8 %copy-start = (f32[6,128,512]{2,1,0:T(8,128)}, f32[6,128,512]{2,1,0:T(8,128)S(1)}, u32[]{:S(2)}) copy-start(f32[6,128,512]{2,1,0:T(8,128)S(1)} %get-tuple-element.211) | copy-start | bytes 4718596 | tf_op jit(solution)/shard_map/while
  121.4 2.8 %copy-start = (f32[6,128,512]{2,1,0:T(8,128)}, f32[6,128,512]{2,1,0:T(8,128)S(1)}, u32[]{:S(2)}) copy-start(f32[6,128,512]{2,1,0:T(8,128)S(1)} %get-tuple-element.211) | copy-start | bytes 4718596 | tf_op jit(solution)/shard_map/while
  128.9 2.8 %copy-start = (f32[6,128,512]{2,1,0:T(8,128)}, f32[6,128,512]{2,1,0:T(8,128)S(1)}, u32[]{:S(2)}) copy-start(f32[6,128,512]{2,1,0:T(8,128)S(1)} %get-tuple-element.211) | copy-start | bytes 4718596 | tf_op jit(solution)/shard_map/while
  137.0 8.5 %all-to-all-start.1 = ((f32[8,8,384]{2,1,0:T(8,128)}), f32[8,8,384]{2,1,0:T(8,128)S(1)}, u32[]{:S(2)}, u32[]{:S(2)}) async-start(f32[8,8,384]{2,1,0:T(8,128)} %bitcast.5), calls=%async_computation.1 | async-start | bytes 196608 | tf_op jit(solution)/shard_map/all_to_all | solution.py:118
  (12 other events, 22.0 us)
Sparse Core Ops, SparseCore 0:
  9.9 28.8 all-gather.1
where the time goes:
time: 174 us; the launch traced here: 173 us
  other arithmetic  81.9 us (47%)
  local copies, waits for them, and re-layouts  24 us (14%)
  blocking collectives  18.7 us (11%)
  waiting for transfers between devices  17.3 us (10%)
  between operations  14.2 us (8%)
  starting transfers between devices  11.9 us (7%)
  matrix products  4.24 us (2%)
    reduce_sum x12, other arithmetic, month_step(): first_state = state[0] * stay_rate[0] + jnp.sum(backward[1:], axis=0)  32.9 us
    dynamic_update_slice x12, other arithmetic, roll_months(): state_pair, history = lax.scan(month_step, (start_state, loss_start), level)  26.6 us
    psum x1, blocking collectives, shards(): expected_loss = lax.psum(partial_value, 'path') / path_count  18.7 us
    sub x12, other arithmetic, month_step(): stay_rate = (1.0 - roll_rate) * (1.0 - cure_rate)  14.8 us
    dynamic_slice x24, local copies, waits for them, and re-layouts, roll_months(): state_pair, history = lax.scan(month_step, (start_state, loss_start), level)  13.2 us
    all_gather x1, waiting for transfers between devices, shards(): shard = lax.all_gather(price_moves, 'loan', axis=1, tiled=True)  6.63 us
    all_to_all x1, starting transfers between devices, shards(): lax.all_to_all(outgoing[2], 'loan', split_axis=0, concat_axis=0, tiled=True)  5.2 us
    all_to_all x1, waiting for transfers between devices, shards(): lax.all_to_all(outgoing[0], 'loan', split_axis=0, concat_axis=0, tiled=True)  4.94 us
  transfers between devices with their start and end apart: 4, of which 4 were waited for; matrix products, arithmetic and copies ran while one was open for 5% of the time, Pallas kernels for 0%

commit v1 on v0

--- a/solution.py
+++ b/solution.py
@@ -136,7 +136,7 @@
     height = (detach - attach).T[:, :, None, None]
     shares = jnp.clip((ratio[None] - lower) / height, 0.0, 1.0)
     partial_value = jnp.sum(shares, axis=3).transpose(0, 2, 1)
-    expected_loss = lax.psum(partial_value, "path") / path_count
+    expected_loss = jnp.sum(lax.all_gather(partial_value, "path"), axis=0) / path_count
     return (expected_loss, shares[:, :, -1, :])
 
 

time: 174 us -> 169 us (0.971)
  blocking collectives: 18.7 us -> 13.2 us
    psum x1 -> x0, blocking collectives: 18.7 us -> none  [shards(): expected_loss = lax.psum(partial_value, 'path') / path_count]
    all_gather x0 -> x1, blocking collectives: none -> 13.2 us  [shards(): lax.all_gather(partial_value, 'path')]
where the time goes in v1:
time: 169 us; the launch traced here: 167 us
  other arithmetic  82.5 us (49%)
  local copies, waits for them, and re-layouts  23.4 us (14%)
  waiting for transfers between devices  17.3 us (10%)
  between operations  14.2 us (8%)
  blocking collectives  13.2 us (8%)
  starting transfers between devices  11.9 us (7%)
  matrix products  4.24 us (3%)
    reduce_sum x12, other arithmetic, month_step(): first_state = state[0] * stay_rate[0] + jnp.sum(backward[1:], axis=0)  32.9 us
    dynamic_update_slice x12, other arithmetic, roll_months(): state_pair, history = lax.scan(month_step, (start_state, loss_start), level)  26.6 us
    sub x12, other arithmetic, month_step(): stay_rate = (1.0 - roll_rate) * (1.0 - cure_rate)  14.8 us
    dynamic_slice x24, local copies, waits for them, and re-layouts, roll_months(): state_pair, history = lax.scan(month_step, (start_state, loss_start), level)  13.2 us
    all_gather x1, blocking collectives, shards(): lax.all_gather(partial_value, 'path')  13.2 us
    all_gather x1, waiting for transfers between devices, shards(): shard = lax.all_gather(price_moves, 'loan', axis=1, tiled=True)  6.63 us
    all_to_all x1, starting transfers between devices, shards(): lax.all_to_all(outgoing[2], 'loan', split_axis=0, concat_axis=0, tiled=True)  5.2 us
    all_to_all x1, waiting for transfers between devices, shards(): lax.all_to_all(outgoing[0], 'loan', split_axis=0, concat_axis=0, tiled=True)  4.94 us
  transfers between devices with their start and end apart: 4, of which 4 were waited for; matrix products, arithmetic and copies ran while one was open for 5% of the time, Pallas kernels for 0%

profile of v1, /device:TPU:0, one launch (start us, length us, event | category | flops | bytes accessed | tf_op | source)
XLA Modules:
  0.0 167.5 jit_solution(10723421372465359828)
XLA Ops:
  13.2 5.2 %all-to-all-start = ((f32[8,8,1]{1,2,0:T(1,128)}), f32[8,8,1]{1,2,0:T(1,128)S(1)}, u32[]{:S(2)}, u32[]{:S(2)}) async-start(f32[8,8,1]{1,2,0:T(1,128)} %bitcast), calls=%async_computation | async-start | bytes 8192 | tf_op jit(solution)/shard_map/all_to_all | solution.py:120
  23.0 3.3 %all-to-all-start.2 = ((f32[8,8,1]{1,2,0:T(1,128)}), f32[8,8,1]{1,2,0:T(1,128)S(1)}, u32[]{:S(2)}, u32[]{:S(2)}) async-start(f32[8,8,1]{1,2,0:T(1,128)} %bitcast.10), calls=%async_computation.2 | async-start | bytes 8192 | tf_op jit(solution)/shard_map/all_to_all | solution.py:119
  26.5 4.4 %all-to-all-done.2 = f32[8,8,1]{1,2,0:T(1,128)S(1)} async-done(((f32[8,8,1]{1,2,0:T(1,128)}), f32[8,8,1]{1,2,0:T(1,128)S(1)}, u32[]{:S(2)}, u32[]{:S(2)}) %all-to-all-start.2) | async-done | bytes 288 | tf_op jit(solution)/shard_map/all_to_all | solution.py:119
  32.2 6.6 %all-gather.3.cloned.1.call-done = bf16[12,416,128]{2,0,1:T(8,128)(2,1)} async-done(((bf16[12,52,128]{2,0,1:T(8,128)(2,1)}), bf16[12,416,128]{2,0,1:T(8,128)(2,1)}) %all-gather.3.cloned.1.call-update) | async-done | bytes 1277968 | tf_op jit(solution)/shard_map/all_gather | solution.py:73
  38.8 2.5 %fusion.9 = f32[512,12,128]{2,0,1:T(8,128)S(1)} fusion(bf16[12,416,128]{2,0,1:T(8,128)(2,1)} %all-gather.3.cloned.1.call-done, s32[512]{0:T(512)S(1)} %select_reduce_fusion), kind=kOutput, calls=%fused_computation.28 | convolution fusion | flops 654524416 | bytes 4425728 | tf_op jit(solution)/shard_map/mrp,rl->mpl/dot_general | solution.py:77
  44.1 89.9 %while.15 = (s32[]{:T(128)}, f32[6,128,512]{2,1,0:T(8,128)S(1)}, f32[128,512]{1,0:T(8,128)}, f32[12,128,512]{2,1,0:T(8,128)}, f32[2,6]{1,0:T(2,128)S(1)}, /*inde...) while((s32[]{:T(128)}, f32[6,128,512]{2,1,0:T(8,128)S(1)}, ...), condition=%wide.region_5.6_spmd.clone, body=%wide.region_3.5_spmd.clone.sunk | while | flops 8257539 | bytes 34343880 | solution.py:43
  46.4 2.7 %fusion.43 = (f32[128,512]{1,0:T(8,128)}, f32[5,128,512]{2,1,0:T(8,128)}) fusion(f32[6,128,512]{2,1,0:T(8,128)S(1)} %get-tuple-element.205, f32[6,128,512]{2,1,0:T(8,128)S(1)} %get-tuple-element.206, f32[6,128,512]{2,1,0:T(8,128)S(1)} %get-tuple-element.225, f32[6,128,512]{2,1,0:T(8,128)S(1)} %get-tuple-element.207, ...), kind=kLoop, calls=%fused_computation.10.clone.1 | loop fusion | flops 1572864 | bytes 8126464 | tf_op jit(solution)/shard_map/while/body/eval_jaxpr/reduce_sum | solution.py:36
  53.9 2.7 %fusion.43 = (f32[128,512]{1,0:T(8,128)}, f32[5,128,512]{2,1,0:T(8,128)}) fusion(f32[6,128,512]{2,1,0:T(8,128)S(1)} %get-tuple-element.205, f32[6,128,512]{2,1,0:T(8,128)S(1)} %get-tuple-element.206, f32[6,128,512]{2,1,0:T(8,128)S(1)} %get-tuple-element.225, f32[6,128,512]{2,1,0:T(8,128)S(1)} %get-tuple-element.207, ...), kind=kLoop, calls=%fused_computation.10.clone.1 | loop fusion | flops 1572864 | bytes 8126464 | tf_op jit(solution)/shard_map/while/body/eval_jaxpr/reduce_sum | solution.py:36
  56.6 2.2 %bitcast_dynamic-update-slice_fusion.2 = (f32[12,128,512]{2,1,0:T(8,128)}, f32[128,512]{1,0:T(8,128)}, f32[1,128,512]{2,1,0:T(8,128)S(1)}) fusion(f32[12,128,512]{2,1,0:T(8,128)} %get-tuple-element.227, s32[]{:T(128)} %get-tuple-element.224, f32[6,128,512]{2,1,0:T(8,128)S(1)} %get-tuple-element.208, f32[1,128,512]{2,1,0:T(8,128)S(1)} %copy.39, ...), kind=kLoop, calls=%fused_computation.19.clone.1 | loop fusion | flops 786432 | bytes 2361857 | tf_op jit(solution)/shard_map/while/body/jit(dynamic_update_index_in_dim)/dynamic_update_slice | solution.py:43
  61.4 2.7 %fusion.43 = (f32[128,512]{1,0:T(8,128)}, f32[5,128,512]{2,1,0:T(8,128)}) fusion(f32[6,128,512]{2,1,0:T(8,128)S(1)} %get-tuple-element.205, f32[6,128,512]{2,1,0:T(8,128)S(1)} %get-tuple-element.206, f32[6,128,512]{2,1,0:T(8,128)S(1)} %get-tuple-element.225, f32[6,128,512]{2,1,0:T(8,128)S(1)} %get-tuple-element.207, ...), kind=kLoop, calls=%fused_computation.10.clone.1 | loop fusion | flops 1572864 | bytes 8126464 | tf_op jit(solution)/shard_map/while/body/eval_jaxpr/reduce_sum | solution.py:36
  68.9 2.7 %fusion.43 = (f32[128,512]{1,0:T(8,128)}, f32[5,128,512]{2,1,0:T(8,128)}) fusion(f32[6,128,512]{2,1,0:T(8,128)S(1)} %get-tuple-element.205, f32[6,128,512]{2,1,0:T(8,128)S(1)} %get-tuple-element.206, f32[6,128,512]{2,1,0:T(8,128)S(1)} %get-tuple-element.225, f32[6,128,512]{2,1,0:T(8,128)S(1)} %get-tuple-element.207, ...), kind=kLoop, calls=%fused_computation.10.clone.1 | loop fusion | flops 1572864 | bytes 8126464 | tf_op jit(solution)/shard_map/while/body/eval_jaxpr/reduce_sum | solution.py:36
  76.4 2.7 %fusion.43 = (f32[128,512]{1,0:T(8,128)}, f32[5,128,512]{2,1,0:T(8,128)}) fusion(f32[6,128,512]{2,1,0:T(8,128)S(1)} %get-tuple-element.205, f32[6,128,512]{2,1,0:T(8,128)S(1)} %get-tuple-element.206, f32[6,128,512]{2,1,0:T(8,128)S(1)} %get-tuple-element.225, f32[6,128,512]{2,1,0:T(8,128)S(1)} %get-tuple-element.207, ...), kind=kLoop, calls=%fused_computation.10.clone.1 | loop fusion | flops 1572864 | bytes 8126464 | tf_op jit(solution)/shard_map/while/body/eval_jaxpr/reduce_sum | solution.py:36
  79.1 2.2 %bitcast_dynamic-update-slice_fusion.2 = (f32[12,128,512]{2,1,0:T(8,128)}, f32[128,512]{1,0:T(8,128)}, f32[1,128,512]{2,1,0:T(8,128)S(1)}) fusion(f32[12,128,512]{2,1,0:T(8,128)} %get-tuple-element.227, s32[]{:T(128)} %get-tuple-element.224, f32[6,128,512]{2,1,0:T(8,128)S(1)} %get-tuple-element.208, f32[1,128,512]{2,1,0:T(8,128)S(1)} %copy.39, ...), kind=kLoop, calls=%fused_computation.19.clone.1 | loop fusion | flops 786432 | bytes 2361857 | tf_op jit(solution)/shard_map/while/body/jit(dynamic_update_index_in_dim)/dynamic_update_slice | solution.py:43
  83.9 2.7 %fusion.43 = (f32[128,512]{1,0:T(8,128)}, f32[5,128,512]{2,1,0:T(8,128)}) fusion(f32[6,128,512]{2,1,0:T(8,128)S(1)} %get-tuple-element.205, f32[6,128,512]{2,1,0:T(8,128)S(1)} %get-tuple-element.206, f32[6,128,512]{2,1,0:T(8,128)S(1)} %get-tuple-element.225, f32[6,128,512]{2,1,0:T(8,128)S(1)} %get-tuple-element.207, ...), kind=kLoop, calls=%fused_computation.10.clone.1 | loop fusion | flops 1572864 | bytes 8126464 | tf_op jit(solution)/shard_map/while/body/eval_jaxpr/reduce_sum | solution.py:36
  91.4 2.7 %fusion.43 = (f32[128,512]{1,0:T(8,128)}, f32[5,128,512]{2,1,0:T(8,128)}) fusion(f32[6,128,512]{2,1,0:T(8,128)S(1)} %get-tuple-element.205, f32[6,128,512]{2,1,0:T(8,128)S(1)} %get-tuple-element.206, f32[6,128,512]{2,1,0:T(8,128)S(1)} %get-tuple-element.225, f32[6,128,512]{2,1,0:T(8,128)S(1)} %get-tuple-element.207, ...), kind=kLoop, calls=%fused_computation.10.clone.1 | loop fusion | flops 1572864 | bytes 8126464 | tf_op jit(solution)/shard_map/while/body/eval_jaxpr/reduce_sum | solution.py:36
  98.9 2.7 %fusion.43 = (f32[128,512]{1,0:T(8,128)}, f32[5,128,512]{2,1,0:T(8,128)}) fusion(f32[6,128,512]{2,1,0:T(8,128)S(1)} %get-tuple-element.205, f32[6,128,512]{2,1,0:T(8,128)S(1)} %get-tuple-element.206, f32[6,128,512]{2,1,0:T(8,128)S(1)} %get-tuple-element.225, f32[6,128,512]{2,1,0:T(8,128)S(1)} %get-tuple-element.207, ...), kind=kLoop, calls=%fused_computation.10.clone.1 | loop fusion | flops 1572864 | bytes 8126464 | tf_op jit(solution)/shard_map/while/body/eval_jaxpr/reduce_sum | solution.py:36
  101.6 2.3 %bitcast_dynamic-update-slice_fusion.2 = (f32[12,128,512]{2,1,0:T(8,128)}, f32[128,512]{1,0:T(8,128)}, f32[1,128,512]{2,1,0:T(8,128)S(1)}) fusion(f32[12,128,512]{2,1,0:T(8,128)} %get-tuple-element.227, s32[]{:T(128)} %get-tuple-element.224, f32[6,128,512]{2,1,0:T(8,128)S(1)} %get-tuple-element.208, f32[1,128,512]{2,1,0:T(8,128)S(1)} %copy.39, ...), kind=kLoop, calls=%fused_computation.19.clone.1 | loop fusion | flops 786432 | bytes 2361857 | tf_op jit(solution)/shard_map/while/body/jit(dynamic_update_index_in_dim)/dynamic_update_slice | solution.py:43
  106.4 2.7 %fusion.43 = (f32[128,512]{1,0:T(8,128)}, f32[5,128,512]{2,1,0:T(8,128)}) fusion(f32[6,128,512]{2,1,0:T(8,128)S(1)} %get-tuple-element.205, f32[6,128,512]{2,1,0:T(8,128)S(1)} %get-tuple-element.206, f32[6,128,512]{2,1,0:T(8,128)S(1)} %get-tuple-element.225, f32[6,128,512]{2,1,0:T(8,128)S(1)} %get-tuple-element.207, ...), kind=kLoop, calls=%fused_computation.10.clone.1 | loop fusion | flops 1572864 | bytes 8126464 | tf_op jit(solution)/shard_map/while/body/eval_jaxpr/reduce_sum | solution.py:36
  113.9 2.7 %fusion.43 = (f32[128,512]{1,0:T(8,128)}, f32[5,128,512]{2,1,0:T(8,128)}) fusion(f32[6,128,512]{2,1,0:T(8,128)S(1)} %get-tuple-element.205, f32[6,128,512]{2,1,0:T(8,128)S(1)} %get-tuple-element.206, f32[6,128,512]{2,1,0:T(8,128)S(1)} %get-tuple-element.225, f32[6,128,512]{2,1,0:T(8,128)S(1)} %get-tuple-element.207, ...), kind=kLoop, calls=%fused_computation.10.clone.1 | loop fusion | flops 1572864 | bytes 8126464 | tf_op jit(solution)/shard_map/while/body/eval_jaxpr/reduce_sum | solution.py:36
  121.4 2.7 %fusion.43 = (f32[128,512]{1,0:T(8,128)}, f32[5,128,512]{2,1,0:T(8,128)}) fusion(f32[6,128,512]{2,1,0:T(8,128)S(1)} %get-tuple-element.205, f32[6,128,512]{2,1,0:T(8,128)S(1)} %get-tuple-element.206, f32[6,128,512]{2,1,0:T(8,128)S(1)} %get-tuple-element.225, f32[6,128,512]{2,1,0:T(8,128)S(1)} %get-tuple-element.207, ...), kind=kLoop, calls=%fused_computation.10.clone.1 | loop fusion | flops 1572864 | bytes 8126464 | tf_op jit(solution)/shard_map/while/body/eval_jaxpr/reduce_sum | solution.py:36
  128.9 2.7 %fusion.43 = (f32[128,512]{1,0:T(8,128)}, f32[5,128,512]{2,1,0:T(8,128)}) fusion(f32[6,128,512]{2,1,0:T(8,128)S(1)} %get-tuple-element.205, f32[6,128,512]{2,1,0:T(8,128)S(1)} %get-tuple-element.206, f32[6,128,512]{2,1,0:T(8,128)S(1)} %get-tuple-element.225, f32[6,128,512]{2,1,0:T(8,128)S(1)} %get-tuple-element.207, ...), kind=kLoop, calls=%fused_computation.10.clone.1 | loop fusion | flops 1572864 | bytes 8126464 | tf_op jit(solution)/shard_map/while/body/eval_jaxpr/reduce_sum | solution.py:36
  137.0 3.4 %all-to-all-start.1 = ((f32[8,8,384]{2,1,0:T(8,128)}), f32[8,8,384]{2,1,0:T(8,128)S(1)}, u32[]{:S(2)}, u32[]{:S(2)}) async-start(f32[8,8,384]{2,1,0:T(8,128)} %bitcast.5), calls=%async_computation.1 | async-start | bytes 196608 | tf_op jit(solution)/shard_map/all_to_all | solution.py:118
  140.6 4.9 %all-to-all-done.1 = f32[8,8,384]{2,1,0:T(8,128)S(1)} async-done(((f32[8,8,384]{2,1,0:T(8,128)}), f32[8,8,384]{2,1,0:T(8,128)S(1)}, u32[]{:S(2)}, u32[]{:S(2)}) %all-to-all-start.1) | async-done | bytes 98336 | tf_op jit(solution)/shard_map/all_to_all | solution.py:118
  146.8 13.2 %all-gather = f32[24,3,64]{2,1,0:T(4,128)S(1)} all-gather(f32[6,3,64]{2,1,0:T(4,128)S(1)} %copy.29), channel_id=2, replica_groups=mesh['loan'=8,'path'=4] {'path'}, dimensions={0}, use_global_device_ids=true | all-gather | bytes 23040 | tf_op jit(solution)/shard_map/all_gather | solution.py:139
  (193 shorter events, 69.3 us)
Async XLA Ops:
  7.2 14.3 %copy-start.9 = (s32[2,32]{1,0:T(2,128)S(1)}, s32[2,32]{1,0:T(2,128)}, u32[]{:S(2)}) copy-start(s32[2,32]{1,0:T(2,128)} %param.14) | copy-start | bytes 772
  7.2 14.3 %copy-start.5 = (s32[64,6]{0,1:T(8,128)S(1)}, s32[64,6]{0,1:T(8,128)}, u32[]{:S(2)}) copy-start(s32[64,6]{0,1:T(8,128)} %param.23) | copy-start | bytes 4612
  7.2 14.4 %copy-start.7 = (s32[512]{0:T(512)S(1)}, s32[512]{0:T(512)}, u32[]{:S(2)}) copy-start(s32[512]{0:T(512)} %param.15) | copy-start | bytes 6148
  7.2 14.6 %copy-start.6 = (s32[512]{0:T(512)S(1)}, s32[512]{0:T(512)}, u32[]{:S(2)}) copy-start(s32[512]{0:T(512)} %param.18) | copy-start | bytes 6148
  7.2 14.6 %copy-start.8 = (f32[512]{0:T(512)S(1)}, f32[512]{0:T(512)}, u32[]{:S(2)}) copy-start(f32[512]{0:T(512)} %param.20) | copy-start | bytes 6148
  7.2 31.6 %all-gather.3.cloned.1.call-start = ((), (), s32[]{:S(2)}) async-start(), calls=%async_computation.3 | async-start | bytes 1916928 | tf_op jit(solution)/shard_map/all_gather | solution.py:73
  13.2 9.8 %all-to-all-start = ((f32[8,8,1]{1,2,0:T(1,128)}), f32[8,8,1]{1,2,0:T(1,128)S(1)}, u32[]{:S(2)}, u32[]{:S(2)}) async-start(f32[8,8,1]{1,2,0:T(1,128)} %bitcast), calls=%async_computation | async-start | bytes 8192 | tf_op jit(solution)/shard_map/all_to_all | solution.py:120
  23.0 7.9 %all-to-all-start.2 = ((f32[8,8,1]{1,2,0:T(1,128)}), f32[8,8,1]{1,2,0:T(1,128)S(1)}, u32[]{:S(2)}, u32[]{:S(2)}) async-start(f32[8,8,1]{1,2,0:T(1,128)} %bitcast.10), calls=%async_computation.2 | async-start | bytes 8192 | tf_op jit(solution)/shard_map/all_to_all | solution.py:119
  46.4 2.8 %copy-start = (f32[6,128,512]{2,1,0:T(8,128)}, f32[6,128,512]{2,1,0:T(8,128)S(1)}, u32[]{:S(2)}) copy-start(f32[6,128,512]{2,1,0:T(8,128)S(1)} %get-tuple-element.207) | copy-start | bytes 4718596 | tf_op jit(solution)/shard_map/while
  53.9 2.8 %copy-start = (f32[6,128,512]{2,1,0:T(8,128)}, f32[6,128,512]{2,1,0:T(8,128)S(1)}, u32[]{:S(2)}) copy-start(f32[6,128,512]{2,1,0:T(8,128)S(1)} %get-tuple-element.207) | copy-start | bytes 4718596 | tf_op jit(solution)/shard_map/while
  56.6 2.2 %copy-start.1 = (f32[5,128,512]{2,1,0:T(8,128)S(1)}, f32[5,128,512]{2,1,0:T(8,128)}, u32[]{:S(2)}) copy-start(f32[5,128,512]{2,1,0:T(8,128)} %get-tuple-element.209) | copy-start | bytes 3932164 | tf_op jit(solution)/shard_map/while
  61.4 2.8 %copy-start = (f32[6,128,512]{2,1,0:T(8,128)}, f32[6,128,512]{2,1,0:T(8,128)S(1)}, u32[]{:S(2)}) copy-start(f32[6,128,512]{2,1,0:T(8,128)S(1)} %get-tuple-element.207) | copy-start | bytes 4718596 | tf_op jit(solution)/shard_map/while
  64.1 2.2 %copy-start.1 = (f32[5,128,512]{2,1,0:T(8,128)S(1)}, f32[5,128,512]{2,1,0:T(8,128)}, u32[]{:S(2)}) copy-start(f32[5,128,512]{2,1,0:T(8,128)} %get-tuple-element.209) | copy-start | bytes 3932164 | tf_op jit(solution)/shard_map/while
  68.9 2.8 %copy-start = (f32[6,128,512]{2,1,0:T(8,128)}, f32[6,128,512]{2,1,0:T(8,128)S(1)}, u32[]{:S(2)}) copy-start(f32[6,128,512]{2,1,0:T(8,128)S(1)} %get-tuple-element.207) | copy-start | bytes 4718596 | tf_op jit(solution)/shard_map/while
  76.4 2.8 %copy-start = (f32[6,128,512]{2,1,0:T(8,128)}, f32[6,128,512]{2,1,0:T(8,128)S(1)}, u32[]{:S(2)}) copy-start(f32[6,128,512]{2,1,0:T(8,128)S(1)} %get-tuple-element.207) | copy-start | bytes 4718596 | tf_op jit(solution)/shard_map/while
  83.9 2.8 %copy-start = (f32[6,128,512]{2,1,0:T(8,128)}, f32[6,128,512]{2,1,0:T(8,128)S(1)}, u32[]{:S(2)}) copy-start(f32[6,128,512]{2,1,0:T(8,128)S(1)} %get-tuple-element.207) | copy-start | bytes 4718596 | tf_op jit(solution)/shard_map/while
  91.4 2.8 %copy-start = (f32[6,128,512]{2,1,0:T(8,128)}, f32[6,128,512]{2,1,0:T(8,128)S(1)}, u32[]{:S(2)}) copy-start(f32[6,128,512]{2,1,0:T(8,128)S(1)} %get-tuple-element.207) | copy-start | bytes 4718596 | tf_op jit(solution)/shard_map/while
  98.9 2.8 %copy-start = (f32[6,128,512]{2,1,0:T(8,128)}, f32[6,128,512]{2,1,0:T(8,128)S(1)}, u32[]{:S(2)}) copy-start(f32[6,128,512]{2,1,0:T(8,128)S(1)} %get-tuple-element.207) | copy-start | bytes 4718596 | tf_op jit(solution)/shard_map/while
  101.6 2.3 %copy-start.1 = (f32[5,128,512]{2,1,0:T(8,128)S(1)}, f32[5,128,512]{2,1,0:T(8,128)}, u32[]{:S(2)}) copy-start(f32[5,128,512]{2,1,0:T(8,128)} %get-tuple-element.209) | copy-start | bytes 3932164 | tf_op jit(solution)/shard_map/while
  106.4 2.8 %copy-start = (f32[6,128,512]{2,1,0:T(8,128)}, f32[6,128,512]{2,1,0:T(8,128)S(1)}, u32[]{:S(2)}) copy-start(f32[6,128,512]{2,1,0:T(8,128)S(1)} %get-tuple-element.207) | copy-start | bytes 4718596 | tf_op jit(solution)/shard_map/while
  113.9 2.8 %copy-start = (f32[6,128,512]{2,1,0:T(8,128)}, f32[6,128,512]{2,1,0:T(8,128)S(1)}, u32[]{:S(2)}) copy-start(f32[6,128,512]{2,1,0:T(8,128)S(1)} %get-tuple-element.207) | copy-start | bytes 4718596 | tf_op jit(solution)/shard_map/while
  121.4 2.8 %copy-start = (f32[6,128,512]{2,1,0:T(8,128)}, f32[6,128,512]{2,1,0:T(8,128)S(1)}, u32[]{:S(2)}) copy-start(f32[6,128,512]{2,1,0:T(8,128)S(1)} %get-tuple-element.207) | copy-start | bytes 4718596 | tf_op jit(solution)/shard_map/while
  128.9 2.8 %copy-start = (f32[6,128,512]{2,1,0:T(8,128)}, f32[6,128,512]{2,1,0:T(8,128)S(1)}, u32[]{:S(2)}) copy-start(f32[6,128,512]{2,1,0:T(8,128)S(1)} %get-tuple-element.207) | copy-start | bytes 4718596 | tf_op jit(solution)/shard_map/while
  137.0 8.5 %all-to-all-start.1 = ((f32[8,8,384]{2,1,0:T(8,128)}), f32[8,8,384]{2,1,0:T(8,128)S(1)}, u32[]{:S(2)}, u32[]{:S(2)}) async-start(f32[8,8,384]{2,1,0:T(8,128)} %bitcast.5), calls=%async_computation.1 | async-start | bytes 196608 | tf_op jit(solution)/shard_map/all_to_all | solution.py:118
  (12 other events, 22.0 us)
Sparse Core Ops, SparseCore 0:
  9.9 28.8 all-gather.2
